TPU v7x, 32 devices: a whole 2x2x4 slice. The times are simulated.
32 devices in a mesh: row: 8 (over z, y), col: 4 (over x, core).
Axes of the slice: x: 2, y: 2, z: 4, core: 2. Of those that a mesh axis runs over, the one named last changes fastest.
Arguments:
- weights: bfloat16 [2, 8192, 8192], P(None, 'row', 'col'), may hold values from -0.0625 to 0.0625
- preact: float32 [2, 2, 8192], P(None, None, 'row'), may hold values from -2.5 to 2.5
- panel: bfloat16 [2, 64, 8192], P(None, None, 'col'), may hold values from -6 to 6
Outputs:
- basis_out: float32 [2, 64, 8192], P(None, None, 'col')
All inputs are finite; a program needn't handle non-finite values.
Results may differ from a plain program's by a relative error of at most 0.035.
Values may be sent and summed in bfloat16 or wider, within the bound.
A program may use at most 64 MiB of HBM per device.

v0:
```python
from functools import partial
import jax
import jax.numpy as jnp
from jax import lax
from jax.sharding import PartitionSpec as P

WIDTH = 8192
ITERS = 2


def on_device(weights, preact, panel):
    slopes = 1.0 - jnp.tanh(preact) ** 2
    layers = weights.shape[0]
    current = panel
    basis_out = panel.astype(jnp.float32)
    for iteration in range(ITERS):
        cotangent = None
        for layer_at in range(layers):
            partial_out = jnp.einsum(
                "bki,oi->bko", current, weights[layer_at], preferred_element_type=jnp.float32
            )
            summed = lax.psum_scatter(
                partial_out.astype(jnp.bfloat16), "col", scatter_dimension=1, tiled=True
            ).astype(jnp.float32)
            scaled = (slopes[:, layer_at, None, :] * summed).astype(jnp.bfloat16)
            if layer_at + 1 < layers:
                spread = lax.all_gather(scaled, "row", axis=2, tiled=True)
                current = lax.all_to_all(spread, "col", split_axis=2, concat_axis=1, tiled=True)
            else:
                cotangent = lax.all_gather(scaled, "col", axis=1, tiled=True)
        image_panel = None
        for layer_at in reversed(range(layers)):
            weighted = (slopes[:, layer_at, None, :] * cotangent).astype(jnp.bfloat16)
            partial_in = jnp.einsum(
                "bko,oi->bki", weighted, weights[layer_at], preferred_element_type=jnp.float32
            )
            if layer_at == 0:
                pieces = lax.psum_scatter(
                    partial_in.astype(jnp.bfloat16), "row", scatter_dimension=2, tiled=True
                )
                image_panel = lax.all_gather(pieces, "row", axis=2, tiled=True)
            else:
                pieces = lax.psum_scatter(
                    partial_in.astype(jnp.bfloat16), "row", scatter_dimension=1, tiled=True
                )
                spread = lax.all_gather(pieces, "col", axis=2, tiled=True)
                cotangent = lax.all_to_all(spread, "row", split_axis=2, concat_axis=1, tiled=True)
        local_gram = jnp.einsum(
            "bkw,bjw->bkj", image_panel, image_panel, preferred_element_type=jnp.float32
        )
        gram_sum = lax.psum(local_gram.astype(jnp.bfloat16), "col").astype(jnp.float32)
        factor = jnp.linalg.cholesky(gram_sum / WIDTH)
        basis_out = jax.vmap(partial(jax.scipy.linalg.solve_triangular, lower=True))(
            factor, image_panel.astype(jnp.float32)
        )
        current = basis_out.astype(jnp.bfloat16)
    return basis_out


def solution(mesh):
    return jax.shard_map(
        on_device,
        mesh=mesh,
        in_specs=(P(None, "row", "col"), P(None, None, "row"), P(None, None, "col")),
        out_specs=P(None, None, "col"),
        check_vma=False,
    )
```

profile of v0, /device:TPU:0, one launch (start us, length us, event | category | flops | bytes accessed | tf_op | source)
XLA Modules:
  0.0 776.8 jit_solution(17862595918340202358)
XLA Ops:
  12.1 22.8 %reduce-scatter.13.cloned.1.call-done = bf16[2,16,1024]{2,1,0:T(8,128)(2,1)} async-done(((bf16[2,64,1024]{2,1,0:T(8,128)(2,1)}), bf16[2,16,1024]{2,1,0:T(8,128)(2,1)}) %reduce-scatter.13.cloned.1.call-update) | async-done | bytes 65552 | tf_op jit(solution)/shard_map/reduce_scatter | solution.py:22
  35.8 31.6 %all_gather.24 = bf16[2,16,8192]{2,1,0:T(8,128)(2,1)S(1)} all-gather(bf16[2,16,1024]{2,1,0:T(8,128)(2,1)S(1)} %multiply_convert_fusion.7), channel_id=1, replica_groups=mesh['row'=8,'col'=4] {'row'}, dimensions={2}, use_global_device_ids=true | all-gather | bytes 589824 | tf_op jit(solution)/shard_map/all_gather | solution.py:27
  79.9 11.2 %all_to_all.54 = bf16[4,2,32768]{2,1,0:T(2,128)(2,1)S(1)} all-to-all(bf16[4,2,32768]{2,1,0:T(2,128)(2,1)S(1)} %reshape.23), channel_id=1, replica_groups=mesh['row'=8,'col'=4] {'col'}, dimensions={0} | all-to-all | bytes 1048576 | tf_op jit(solution)/shard_map/all_to_all | solution.py:28
  95.2 9.7 %copy.67 = bf16[2,16,4,2048]{3,2,1,0:T(4,128)(2,1)S(1)} copy(bf16[2,16,4,2048]{1,0,3,2:T(2,128)(2,1)} %bitcast.105) | data formatting | bytes 1048576 | tf_op jit(solution)/shard_map/all_to_all | solution.py:28
  109.7 20.0 %reduce-scatter.15.cloned.1.call-done = bf16[2,16,1024]{2,1,0:T(8,128)(2,1)} async-done(((bf16[2,64,1024]{2,1,0:T(8,128)(2,1)}), bf16[2,16,1024]{2,1,0:T(8,128)(2,1)}) %reduce-scatter.15.cloned.1.call-update) | async-done | bytes 65552 | tf_op jit(solution)/shard_map/reduce_scatter | solution.py:22
  140.9 63.2 %reduce-scatter.25.cloned.1.call-done = bf16[8,4096]{1,0:T(8,128)(2,1)} async-done(((bf16[64,4096]{1,0:T(8,128)(2,1)}), bf16[8,4096]{1,0:T(8,128)(2,1)}) %reduce-scatter.25.cloned.1.call-update) | async-done | bytes 65552
  227.8 9.0 %all-to-all-done.1 = bf16[8,2,8192]{2,1,0:T(2,128)(2,1)S(1)} async-done(((bf16[8,2,8192]{2,1,0:T(2,128)(2,1)}), bf16[8,2,8192]{2,1,0:T(2,128)(2,1)S(1)}, u32[]{:S(2)}, u32[]{:S(2)}) %all-to-all-start.1) | async-done | bytes 262176 | tf_op jit(solution)/shard_map/all_to_all | solution.py:47
  263.0 62.1 %reduce-scatter.17.cloned.1.call-done = bf16[2,64,256]{2,1,0:T(8,128)(2,1)} async-done(((bf16[2,64,2048]{2,1,0:T(8,128)(2,1)}), bf16[2,64,256]{2,1,0:T(8,128)(2,1)}) %reduce-scatter.17.cloned.1.call-update) | async-done | bytes 65552 | tf_op jit(solution)/shard_map/reduce_scatter | solution.py:38
  325.1 31.8 %all_gather.27 = bf16[2,64,2048]{2,1,0:T(8,128)(2,1)S(1)} all-gather(bf16[2,64,256]{2,1,0:T(8,128)(2,1)} %reduce-scatter.17.cloned.1.call-done), channel_id=1, replica_groups=mesh['row'=8,'col'=4] {'row'}, dimensions={2}, use_global_device_ids=true | all-gather | bytes 589824 | tf_op jit(solution)/shard_map/all_gather | solution.py:41
  357.2 10.3 %psum.14 = bf16[2,64,64]{1,2,0:T(8,128)(2,1)S(1)} all-reduce(bf16[2,64,64]{1,2,0:T(8,128)(2,1)S(1)} %convolution_convert_fusion.2), channel_id=1, replica_groups=mesh['row'=8,'col'=4] {'col'}, use_global_device_ids=true, to_apply=%region_4.0 | all-reduce | flops 8192 | bytes 32768 | tf_op jit(solution)/shard_map/psum | solution.py:51
  367.6 11.7 %custom-call.8 = f32[2,64,64]{2,1,0:T(8,128)S(1)} custom-call(f32[2,64,64]{2,1,0:T(8,128)S(1)} %fusion.62), custom_call_target="Cholesky" | custom-call | tf_op jit(solution)/shard_map/jit(cholesky)/cholesky | solution.py:52
  379.6 9.8 %custom-call.9 = f32[2,1,64,64]{2,3,1,0:T(8,128)S(1)} custom-call(f32[2,1,64,64]{3,2,1,0:T(8,128)S(1)} %select_bitcast_fusion.1), custom_call_target="InvertDiagBlocksLowerTriangular" | custom-call | tf_op jit(solution)/shard_map/vmap(jit(_solve_triangular))/triangular_solve | solution.py:53
  395.0 19.1 %reduce-scatter.19.cloned.1.call-done = bf16[2,16,1024]{2,1,0:T(8,128)(2,1)} async-done(((bf16[2,64,1024]{2,1,0:T(8,128)(2,1)}), bf16[2,16,1024]{2,1,0:T(8,128)(2,1)}) %reduce-scatter.19.cloned.1.call-update) | async-done | bytes 65552 | tf_op jit(solution)/shard_map/reduce_scatter | solution.py:22
  414.9 31.5 %all_gather.28 = bf16[2,16,8192]{2,1,0:T(8,128)(2,1)S(1)} all-gather(bf16[2,16,1024]{2,1,0:T(8,128)(2,1)S(1)} %multiply_convert_fusion.5), channel_id=1, replica_groups=mesh['row'=8,'col'=4] {'row'}, dimensions={2}, use_global_device_ids=true | all-gather | bytes 589824 | tf_op jit(solution)/shard_map/all_gather | solution.py:27
  458.8 11.2 %all_to_all.55 = bf16[4,2,32768]{2,1,0:T(2,128)(2,1)S(1)} all-to-all(bf16[4,2,32768]{2,1,0:T(2,128)(2,1)S(1)} %reshape.27), channel_id=1, replica_groups=mesh['row'=8,'col'=4] {'col'}, dimensions={0} | all-to-all | bytes 1048576 | tf_op jit(solution)/shard_map/all_to_all | solution.py:28
  474.2 9.7 %copy.68 = bf16[2,16,4,2048]{3,2,1,0:T(4,128)(2,1)S(1)} copy(bf16[2,16,4,2048]{1,0,3,2:T(2,128)(2,1)} %bitcast.107) | data formatting | bytes 1048576 | tf_op jit(solution)/shard_map/all_to_all | solution.py:28
  488.7 20.2 %reduce-scatter.21.cloned.1.call-done = bf16[2,16,1024]{2,1,0:T(8,128)(2,1)} async-done(((bf16[2,64,1024]{2,1,0:T(8,128)(2,1)}), bf16[2,16,1024]{2,1,0:T(8,128)(2,1)}) %reduce-scatter.21.cloned.1.call-update) | async-done | bytes 65552 | tf_op jit(solution)/shard_map/reduce_scatter | solution.py:22
  520.0 63.2 %reduce-scatter.27.cloned.1.call-done = bf16[8,4096]{1,0:T(8,128)(2,1)} async-done(((bf16[64,4096]{1,0:T(8,128)(2,1)}), bf16[8,4096]{1,0:T(8,128)(2,1)}) %reduce-scatter.27.cloned.1.call-update) | async-done | bytes 65552
  602.3 12.8 %all_to_all.56 = bf16[8,2,8192]{2,1,0:T(2,128)(2,1)S(1)} all-to-all(bf16[8,2,8192]{2,1,0:T(2,128)(2,1)S(1)} %reshape.29), channel_id=1, replica_groups=mesh['row'=8,'col'=4] {'row'}, dimensions={0} | all-to-all | bytes 524288 | tf_op jit(solution)/shard_map/all_to_all | solution.py:47
  641.3 62.3 %reduce-scatter.23.cloned.1.call-done = bf16[2,64,256]{2,1,0:T(8,128)(2,1)} async-done(((bf16[2,64,2048]{2,1,0:T(8,128)(2,1)}), bf16[2,64,256]{2,1,0:T(8,128)(2,1)}) %reduce-scatter.23.cloned.1.call-update) | async-done | bytes 65552 | tf_op jit(solution)/shard_map/reduce_scatter | solution.py:38
  703.6 31.6 %all_gather.31 = bf16[2,64,2048]{2,1,0:T(8,128)(2,1)S(1)} all-gather(bf16[2,64,256]{2,1,0:T(8,128)(2,1)} %reduce-scatter.23.cloned.1.call-done), channel_id=1, replica_groups=mesh['row'=8,'col'=4] {'row'}, dimensions={2}, use_global_device_ids=true | all-gather | bytes 589824 | tf_op jit(solution)/shard_map/all_gather | solution.py:41
  735.5 10.5 %psum.15 = bf16[2,64,64]{1,2,0:T(8,128)(2,1)S(1)} all-reduce(bf16[2,64,64]{1,2,0:T(8,128)(2,1)S(1)} %convolution_convert_fusion.1), channel_id=1, replica_groups=mesh['row'=8,'col'=4] {'col'}, use_global_device_ids=true, to_apply=%region_11.14 | all-reduce | flops 8192 | bytes 32768 | tf_op jit(solution)/shard_map/psum | solution.py:51
  746.2 11.7 %custom-call.10 = f32[2,64,64]{2,1,0:T(8,128)S(1)} custom-call(f32[2,64,64]{2,1,0:T(8,128)S(1)} %fusion.60), custom_call_target="Cholesky" | custom-call | tf_op jit(solution)/shard_map/jit(cholesky)/cholesky | solution.py:52
  758.1 9.8 %custom-call.11 = f32[2,1,64,64]{2,3,1,0:T(8,128)S(1)} custom-call(f32[2,1,64,64]{3,2,1,0:T(8,128)S(1)} %select_bitcast_fusion), custom_call_target="InvertDiagBlocksLowerTriangular" | custom-call | tf_op jit(solution)/shard_map/vmap(jit(_solve_triangular))/triangular_solve | solution.py:53
  (88 shorter events, 176.0 us)
Async XLA Ops:
  6.5 1.0 copy-start
  6.5 5.5 copy-start.2
  6.5 28.4 %reduce-scatter.13.cloned.1.call-start = ((), (), s32[]{:S(2)}) async-start(), calls=%async_computation.12 | async-start | bytes 327680 | tf_op jit(solution)/shard_map/reduce_scatter | solution.py:22
  12.0 117.8 %reduce-scatter.15.cloned.1.call-start = ((), (), s32[]{:S(2)}) async-start(), calls=%async_computation.13 | async-start | bytes 327680 | tf_op jit(solution)/shard_map/reduce_scatter | solution.py:22
  109.7 94.4 %reduce-scatter.25.cloned.1.call-start = ((), (), s32[]{:S(2)}) async-start(), calls=%async_computation.18 | async-start | bytes 589824
  223.8 13.1 %all-to-all-start.1 = ((bf16[8,2,8192]{2,1,0:T(2,128)(2,1)}), bf16[8,2,8192]{2,1,0:T(2,128)(2,1)S(1)}, u32[]{:S(2)}, u32[]{:S(2)}) async-start(bf16[8,2,8192]{2,1,0:T(2,128)(2,1)} %reshape.25), calls=%async_computation.3 | async-start | bytes 524288 | tf_op jit(solution)/shard_map/all_to_all | solution.py:47
  227.4 97.7 %reduce-scatter.17.cloned.1.call-start = ((), (), s32[]{:S(2)}) async-start(), calls=%async_computation.14 | async-start | bytes 589824 | tf_op jit(solution)/shard_map/reduce_scatter | solution.py:38
  262.9 151.1 %reduce-scatter.19.cloned.1.call-start = ((), (), s32[]{:S(2)}) async-start(), calls=%async_computation.15 | async-start | bytes 327680 | tf_op jit(solution)/shard_map/reduce_scatter | solution.py:22
  394.9 113.9 %reduce-scatter.21.cloned.1.call-start = ((), (), s32[]{:S(2)}) async-start(), calls=%async_computation.16 | async-start | bytes 327680 | tf_op jit(solution)/shard_map/reduce_scatter | solution.py:22
  488.6 94.6 %reduce-scatter.27.cloned.1.call-start = ((), (), s32[]{:S(2)}) async-start(), calls=%async_computation.19 | async-start | bytes 589824
  519.9 183.6 %reduce-scatter.23.cloned.1.call-start = ((), (), s32[]{:S(2)}) async-start(), calls=%async_computation.17 | async-start | bytes 589824 | tf_op jit(solution)/shard_map/reduce_scatter | solution.py:38
  637.5 132.5 %copy-start.1 = (bf16[2,64,2048]{2,1,0:T(8,128)(2,1)S(1)}, bf16[2,64,2048]{2,1,0:T(8,128)(2,1)}, u32[]{:S(2)}) copy-start(bf16[2,64,2048]{2,1,0:T(8,128)(2,1)} %param.8) | copy-start | bytes 1572868
Sparse Core Ops, SparseCore 0:
  12.1 22.7 reduce-scatter.12
  109.8 19.9 reduce-scatter.14
  141.0 63.0 reduce-scatter.24
  263.1 62.0 reduce-scatter.16
  395.0 18.9 reduce-scatter.18
  488.7 20.0 reduce-scatter.20
  520.1 63.1 reduce-scatter.26
  641.4 62.1 reduce-scatter.22
where the time goes:
time: 779 us; the launch traced here: 777 us
  waiting for transfers between devices  342 us (44%)
  blocking collectives  206 us (26%)
  local copies, waits for them, and re-layouts  114 us (15%)
  other arithmetic  62.1 us (8%)
  matrix products  34.7 us (4%)
  between operations  13.8 us (2%)
    unnamed x10, waiting for transfers between devices  127 us
    reduce_scatter x2, waiting for transfers between devices, on_device(): lax.psum_scatter(partial_in.astype(jnp.bfloat16), 'row', scatter_dimensio...  124 us
    reduce_scatter x4, waiting for transfers between devices, on_device(): lax.psum_scatter(partial_out.astype(jnp.bfloat16), 'col', scatter_dimensi...  82.1 us
    all_gather x2, blocking collectives, on_device(): image_panel = lax.all_gather(pieces, 'row', axis=2, tiled=True)  63.4 us
    all_gather x2, blocking collectives, on_device(): spread = lax.all_gather(scaled, 'row', axis=2, tiled=True)  63.1 us
    unnamed x24, local copies, waits for them, and re-layouts  49.6 us
    another operation x7, other arithmetic, on_device(): factor = jnp.linalg.cholesky(gram_sum / WIDTH)  23.8 us
    all_to_all x2, blocking collectives, on_device(): lax.all_to_all(spread, 'col', split_axis=2, concat_axis=1, tiled=True)  22.4 us
  transfers between devices with their start and end apart: 9, of which 9 were waited for; matrix products, arithmetic and copies ran while one was open for 0% of the time, Pallas kernels for 0%

commit v1 on v0

--- a/solution.py
+++ b/solution.py
@@ -6,6 +6,17 @@
 
 WIDTH = 8192
 ITERS = 2
+
+
+def gather_by_hops(block, axis, d):
+    size = lax.axis_size(axis)
+    forward = [(i, (i + 1) % size) for i in range(size)]
+    pieces = [block]
+    for far in range(1, size):
+        pieces = [lax.ppermute(pieces[0], axis, forward), *pieces]
+    whole = jnp.concatenate(pieces, axis=d)
+    shift = (lax.axis_index(axis) + 1) * pieces[-1].shape[d]
+    return jnp.roll(whole, shift, axis=d)
 
 
 def on_device(weights, preact, panel):
@@ -24,7 +35,7 @@
             ).astype(jnp.float32)
             scaled = (slopes[:, layer_at, None, :] * summed).astype(jnp.bfloat16)
             if layer_at + 1 < layers:
-                spread = lax.all_gather(scaled, "row", axis=2, tiled=True)
+                spread = gather_by_hops(scaled, "row", 2)
                 current = lax.all_to_all(spread, "col", split_axis=2, concat_axis=1, tiled=True)
             else:
                 cotangent = lax.all_gather(scaled, "col", axis=1, tiled=True)

time: 779 us -> 818 us (1.050)
  waiting for transfers between devices: 342 us -> 430 us
  blocking collectives: 206 us -> 142 us
    ppermute x0 -> x14, waiting for transfers between devices: none -> 95.6 us  [gather_by_hops(): pieces = [lax.ppermute(pieces[0], axis, forward), *pieces]]
    all_gather x2 -> x0, blocking collectives: 63.1 us -> none  [on_device(): spread = lax.all_gather(scaled, 'row', axis=2, tiled=True)]
    dynamic_slice x0 -> x2, local copies, waits for them, and re-layouts: none -> 13.4 us  [gather_by_hops(): return jnp.roll(whole, shift, axis=d)]
    all_gather x2 -> x0, local copies, waits for them, and re-layouts: 13.4 us -> none  [on_device(): spread = lax.all_gather(scaled, 'row', axis=2, tiled=True)]
    unnamed x24 -> x38, local copies, waits for them, and re-layouts: 49.6 us -> 49.7 us
  transfers between devices with their start and end apart: 9 -> 23, of which waited for: 9 -> 23; matrix products, arithmetic and copies ran while one was open for 0% -> 0% of each run, Pallas kernels for 0% -> 0%
where the time goes in v1:
time: 818 us; the launch traced here: 808 us
  waiting for transfers between devices  430 us (53%)
  blocking collectives  142 us (17%)
  local copies, waits for them, and re-layouts  115 us (14%)
  other arithmetic  64.8 us (8%)
  matrix products  34.7 us (4%)
  between operations  14.2 us (2%)
    unnamed x10, waiting for transfers between devices  127 us
    reduce_scatter x2, waiting for transfers between devices, on_device(): lax.psum_scatter(partial_in.astype(jnp.bfloat16), 'row', scatter_dimensio...  125 us
    ppermute x14, waiting for transfers between devices, gather_by_hops(): pieces = [lax.ppermute(pieces[0], axis, forward), *pieces]  95.6 us
    reduce_scatter x4, waiting for transfers between devices, on_device(): lax.psum_scatter(partial_out.astype(jnp.bfloat16), 'col', scatter_dimensi...  74.7 us
    all_gather x2, blocking collectives, on_device(): image_panel = lax.all_gather(pieces, 'row', axis=2, tiled=True)  63.4 us
    unnamed x38, local copies, waits for them, and re-layouts  49.7 us
    another operation x7, other arithmetic, on_device(): factor = jnp.linalg.cholesky(gram_sum / WIDTH)  23.8 us
    all_to_all x2, blocking collectives, on_device(): lax.all_to_all(spread, 'col', split_axis=2, concat_axis=1, tiled=True)  22.4 us
  transfers between devices with their start and end apart: 23, of which 23 were waited for; matrix products, arithmetic and copies ran while one was open for 0% of the time, Pallas kernels for 0%

profile of v1, /device:TPU:0, one launch (start us, length us, event | category | flops | bytes accessed | tf_op | source)
XLA Modules:
  0.0 808.3 jit_solution(4975356674847637902)
XLA Ops:
  12.1 22.8 %reduce-scatter.13.cloned.1.call-done = bf16[2,16,1024]{2,1,0:T(8,128)(2,1)} async-done(((bf16[2,64,1024]{2,1,0:T(8,128)(2,1)}), bf16[2,16,1024]{2,1,0:T(8,128)(2,1)}) %reduce-scatter.13.cloned.1.call-update) | async-done | bytes 65552 | tf_op jit(solution)/shard_map/reduce_scatter | solution.py:33
  99.1 11.2 %all_to_all.54 = bf16[4,2,32768]{2,1,0:T(2,128)(2,1)S(1)} all-to-all(bf16[4,2,32768]{2,1,0:T(2,128)(2,1)S(1)} %reshape.23), channel_id=1, replica_groups=mesh['row'=8,'col'=4] {'col'}, dimensions={0} | all-to-all | bytes 1048576 | tf_op jit(solution)/shard_map/all_to_all | solution.py:39
  114.4 9.7 %copy.67 = bf16[2,16,4,2048]{3,2,1,0:T(4,128)(2,1)S(1)} copy(bf16[2,16,4,2048]{1,0,3,2:T(2,128)(2,1)} %bitcast.105) | data formatting | bytes 1048576 | tf_op jit(solution)/shard_map/all_to_all | solution.py:39
  128.9 16.3 %reduce-scatter.15.cloned.1.call-done = bf16[2,16,1024]{2,1,0:T(8,128)(2,1)} async-done(((bf16[2,64,1024]{2,1,0:T(8,128)(2,1)}), bf16[2,16,1024]{2,1,0:T(8,128)(2,1)}) %reduce-scatter.15.cloned.1.call-update) | async-done | bytes 65552 | tf_op jit(solution)/shard_map/reduce_scatter | solution.py:33
  156.3 63.2 %reduce-scatter.25.cloned.1.call-done = bf16[8,4096]{1,0:T(8,128)(2,1)} async-done(((bf16[64,4096]{1,0:T(8,128)(2,1)}), bf16[8,4096]{1,0:T(8,128)(2,1)}) %reduce-scatter.25.cloned.1.call-update) | async-done | bytes 65552
  243.6 8.7 %all-to-all-done.1 = bf16[8,2,8192]{2,1,0:T(2,128)(2,1)S(1)} async-done(((bf16[8,2,8192]{2,1,0:T(2,128)(2,1)}), bf16[8,2,8192]{2,1,0:T(2,128)(2,1)S(1)}, u32[]{:S(2)}, u32[]{:S(2)}) %all-to-all-start.1) | async-done | bytes 262176 | tf_op jit(solution)/shard_map/all_to_all | solution.py:58
  265.8 8.9 %copy.51 = bf16[2,8,8,1024]{3,2,1,0:T(8,128)(2,1)S(1)} copy(bf16[2,8,8,1024]{2,0,3,1:T(2,128)(2,1)} %fusion.2) | data formatting | bytes 524288 | tf_op jit(solution)/shard_map/convert_element_type | solution.py:44
  278.5 62.2 %reduce-scatter.17.cloned.1.call-done = bf16[2,64,256]{2,1,0:T(8,128)(2,1)} async-done(((bf16[2,64,2048]{2,1,0:T(8,128)(2,1)}), bf16[2,64,256]{2,1,0:T(8,128)(2,1)}) %reduce-scatter.17.cloned.1.call-update) | async-done | bytes 65552 | tf_op jit(solution)/shard_map/reduce_scatter | solution.py:49
  340.7 31.7 %all_gather.20 = bf16[2,64,2048]{2,1,0:T(8,128)(2,1)S(1)} all-gather(bf16[2,64,256]{2,1,0:T(8,128)(2,1)} %reduce-scatter.17.cloned.1.call-done), channel_id=1, replica_groups=mesh['row'=8,'col'=4] {'row'}, dimensions={2}, use_global_device_ids=true | all-gather | bytes 589824 | tf_op jit(solution)/shard_map/all_gather | solution.py:52
  372.7 10.3 %psum.14 = bf16[2,64,64]{1,2,0:T(8,128)(2,1)S(1)} all-reduce(bf16[2,64,64]{1,2,0:T(8,128)(2,1)S(1)} %convolution_convert_fusion.2), channel_id=1, replica_groups=mesh['row'=8,'col'=4] {'col'}, use_global_device_ids=true, to_apply=%region_4.6 | all-reduce | flops 8192 | bytes 32768 | tf_op jit(solution)/shard_map/psum | solution.py:62
  383.1 11.7 %custom-call.8 = f32[2,64,64]{2,1,0:T(8,128)S(1)} custom-call(f32[2,64,64]{2,1,0:T(8,128)S(1)} %fusion.64), custom_call_target="Cholesky" | custom-call | tf_op jit(solution)/shard_map/jit(cholesky)/cholesky | solution.py:63
  395.1 9.8 %custom-call.9 = f32[2,1,64,64]{2,3,1,0:T(8,128)S(1)} custom-call(f32[2,1,64,64]{3,2,1,0:T(8,128)S(1)} %select_bitcast_fusion.1), custom_call_target="InvertDiagBlocksLowerTriangular" | custom-call | tf_op jit(solution)/shard_map/vmap(jit(_solve_triangular))/triangular_solve | solution.py:64
  410.5 19.2 %reduce-scatter.19.cloned.1.call-done = bf16[2,16,1024]{2,1,0:T(8,128)(2,1)} async-done(((bf16[2,64,1024]{2,1,0:T(8,128)(2,1)}), bf16[2,16,1024]{2,1,0:T(8,128)(2,1)}) %reduce-scatter.19.cloned.1.call-update) | async-done | bytes 65552 | tf_op jit(solution)/shard_map/reduce_scatter | solution.py:33
  494.0 11.2 %all_to_all.55 = bf16[4,2,32768]{2,1,0:T(2,128)(2,1)S(1)} all-to-all(bf16[4,2,32768]{2,1,0:T(2,128)(2,1)S(1)} %reshape.27), channel_id=1, replica_groups=mesh['row'=8,'col'=4] {'col'}, dimensions={0} | all-to-all | bytes 1048576 | tf_op jit(solution)/shard_map/all_to_all | solution.py:39
  509.4 9.7 %copy.68 = bf16[2,16,4,2048]{3,2,1,0:T(4,128)(2,1)S(1)} copy(bf16[2,16,4,2048]{1,0,3,2:T(2,128)(2,1)} %bitcast.107) | data formatting | bytes 1048576 | tf_op jit(solution)/shard_map/all_to_all | solution.py:39
  523.8 16.3 %reduce-scatter.21.cloned.1.call-done = bf16[2,16,1024]{2,1,0:T(8,128)(2,1)} async-done(((bf16[2,64,1024]{2,1,0:T(8,128)(2,1)}), bf16[2,16,1024]{2,1,0:T(8,128)(2,1)}) %reduce-scatter.21.cloned.1.call-update) | async-done | bytes 65552 | tf_op jit(solution)/shard_map/reduce_scatter | solution.py:33
  551.3 63.2 %reduce-scatter.27.cloned.1.call-done = bf16[8,4096]{1,0:T(8,128)(2,1)} async-done(((bf16[64,4096]{1,0:T(8,128)(2,1)}), bf16[8,4096]{1,0:T(8,128)(2,1)}) %reduce-scatter.27.cloned.1.call-update) | async-done | bytes 65552
  633.6 13.0 %all_to_all.56 = bf16[8,2,8192]{2,1,0:T(2,128)(2,1)S(1)} all-to-all(bf16[8,2,8192]{2,1,0:T(2,128)(2,1)S(1)} %reshape.29), channel_id=1, replica_groups=mesh['row'=8,'col'=4] {'row'}, dimensions={0} | all-to-all | bytes 524288 | tf_op jit(solution)/shard_map/all_to_all | solution.py:58
  660.1 8.9 %copy.59 = bf16[2,8,8,1024]{3,2,1,0:T(8,128)(2,1)S(1)} copy(bf16[2,8,8,1024]{2,0,3,1:T(2,128)(2,1)} %fusion.3) | data formatting | bytes 524288 | tf_op jit(solution)/shard_map/convert_element_type | solution.py:44
  672.8 62.3 %reduce-scatter.23.cloned.1.call-done = bf16[2,64,256]{2,1,0:T(8,128)(2,1)} async-done(((bf16[2,64,2048]{2,1,0:T(8,128)(2,1)}), bf16[2,64,256]{2,1,0:T(8,128)(2,1)}) %reduce-scatter.23.cloned.1.call-update) | async-done | bytes 65552 | tf_op jit(solution)/shard_map/reduce_scatter | solution.py:49
  735.1 31.7 %all_gather.23 = bf16[2,64,2048]{2,1,0:T(8,128)(2,1)S(1)} all-gather(bf16[2,64,256]{2,1,0:T(8,128)(2,1)} %reduce-scatter.23.cloned.1.call-done), channel_id=1, replica_groups=mesh['row'=8,'col'=4] {'row'}, dimensions={2}, use_global_device_ids=true | all-gather | bytes 589824 | tf_op jit(solution)/shard_map/all_gather | solution.py:52
  767.0 10.3 %psum.15 = bf16[2,64,64]{1,2,0:T(8,128)(2,1)S(1)} all-reduce(bf16[2,64,64]{1,2,0:T(8,128)(2,1)S(1)} %convolution_convert_fusion.1), channel_id=1, replica_groups=mesh['row'=8,'col'=4] {'col'}, use_global_device_ids=true, to_apply=%region_11.15 | all-reduce | flops 8192 | bytes 32768 | tf_op jit(solution)/shard_map/psum | solution.py:62
  777.4 11.7 %custom-call.10 = f32[2,64,64]{2,1,0:T(8,128)S(1)} custom-call(f32[2,64,64]{2,1,0:T(8,128)S(1)} %fusion.62), custom_call_target="Cholesky" | custom-call | tf_op jit(solution)/shard_map/jit(cholesky)/cholesky | solution.py:63
  789.4 9.8 %custom-call.11 = f32[2,1,64,64]{2,3,1,0:T(8,128)S(1)} custom-call(f32[2,1,64,64]{3,2,1,0:T(8,128)S(1)} %select_bitcast_fusion), custom_call_target="InvertDiagBlocksLowerTriangular" | custom-call | tf_op jit(solution)/shard_map/vmap(jit(_solve_triangular))/triangular_solve | solution.py:64
  (132 shorter events, 260.2 us)
Async XLA Ops:
  6.5 28.4 %reduce-scatter.13.cloned.1.call-start = ((), (), s32[]{:S(2)}) async-start(), calls=%async_computation.12 | async-start | bytes 327680 | tf_op jit(solution)/shard_map/reduce_scatter | solution.py:33
  12.0 133.2 %reduce-scatter.15.cloned.1.call-start = ((), (), s32[]{:S(2)}) async-start(), calls=%async_computation.13 | async-start | bytes 327680 | tf_op jit(solution)/shard_map/reduce_scatter | solution.py:33
  35.8 7.0 collective-permute-start
  42.8 7.0 collective-permute-start.1
  49.8 7.0 collective-permute-start.2
  56.7 7.0 collective-permute-start.3
  63.7 7.5 collective-permute-start.4
  71.2 7.0 collective-permute-start.5
  78.2 7.0 collective-permute-start.6
  128.8 90.7 %reduce-scatter.25.cloned.1.call-start = ((), (), s32[]{:S(2)}) async-start(), calls=%async_computation.18 | async-start | bytes 589824
  239.3 13.1 %all-to-all-start.1 = ((bf16[8,2,8192]{2,1,0:T(2,128)(2,1)}), bf16[8,2,8192]{2,1,0:T(2,128)(2,1)S(1)}, u32[]{:S(2)}, u32[]{:S(2)}) async-start(bf16[8,2,8192]{2,1,0:T(2,128)(2,1)} %reshape.25), calls=%async_computation.3 | async-start | bytes 524288 | tf_op jit(solution)/shard_map/all_to_all | solution.py:58
  242.9 97.8 %reduce-scatter.17.cloned.1.call-start = ((), (), s32[]{:S(2)}) async-start(), calls=%async_computation.14 | async-start | bytes 589824 | tf_op jit(solution)/shard_map/reduce_scatter | solution.py:49
  278.4 151.4 %reduce-scatter.19.cloned.1.call-start = ((), (), s32[]{:S(2)}) async-start(), calls=%async_computation.15 | async-start | bytes 327680 | tf_op jit(solution)/shard_map/reduce_scatter | solution.py:33
  410.5 129.7 %reduce-scatter.21.cloned.1.call-start = ((), (), s32[]{:S(2)}) async-start(), calls=%async_computation.16 | async-start | bytes 327680 | tf_op jit(solution)/shard_map/reduce_scatter | solution.py:33
  430.6 7.0 collective-permute-start.7
  437.6 7.0 collective-permute-start.8
  444.6 7.0 collective-permute-start.9
  451.6 7.0 collective-permute-start.10
  458.5 7.5 collective-permute-start.11
  466.1 7.0 collective-permute-start.12
  473.0 7.1 collective-permute-start.13
  523.8 90.7 %reduce-scatter.27.cloned.1.call-start = ((), (), s32[]{:S(2)}) async-start(), calls=%async_computation.19 | async-start | bytes 589824
  551.3 183.8 %reduce-scatter.23.cloned.1.call-start = ((), (), s32[]{:S(2)}) async-start(), calls=%async_computation.17 | async-start | bytes 589824 | tf_op jit(solution)/shard_map/reduce_scatter | solution.py:49
  669.0 132.3 %copy-start.1 = (bf16[2,64,2048]{2,1,0:T(8,128)(2,1)S(1)}, bf16[2,64,2048]{2,1,0:T(8,128)(2,1)}, u32[]{:S(2)}) copy-start(bf16[2,64,2048]{2,1,0:T(8,128)(2,1)} %param.10) | copy-start | bytes 1572868
  (2 other events, 6.6 us)
Sparse Core Ops, SparseCore 0:
  12.1 22.7 reduce-scatter.12
  129.0 16.2 reduce-scatter.14
  156.4 63.0 reduce-scatter.24
  278.5 62.1 reduce-scatter.16
  410.6 19.1 reduce-scatter.18
  523.9 16.2 reduce-scatter.20
  551.4 63.0 reduce-scatter.26
  672.9 62.1 reduce-scatter.22
